TPU v7x, 32 devices: a whole 2x2x4 slice. The times are simulated.
32 devices in a mesh: groups: 2 (over y), tile: 4 (over z), col: 2 (over x), branch: 2 (over core).
Axes of the slice: x: 2, y: 2, z: 4, core: 2. Of those that a mesh axis runs over, the one named last changes fastest.
Arguments:
- alignment_tensor: float32 [4, 64, 256, 256], P(('groups', 'branch'), 'tile', 'col'), parts along dimension 0, may hold values from -6 to 6
- residue_grid: float32 [4, 256, 256, 128], P(('groups', 'branch'), 'tile', 'col'), parts along dimension 0, may hold values from -6 to 6
- mixing_scale_vector: float32 [256], replicated, may hold values from 0.1 to 1.9
- logit_offset_scale: float32 [128], replicated, may hold values from 0.1 to 1.9
- feedforward_scale: float32 [256], replicated, may hold values from 0.1 to 1.9
- product_scale_vector: float32 [256], replicated, may hold values from 0.1 to 1.9
- grid_scale_vector: float32 [128], replicated, may hold values from 0.1 to 1.9
- logit_offset_map: float32 [128, 8], replicated, may hold values from -0.5 to 0.5
- asking_mapping: bfloat16 [256, 256], replicated, may hold values from -0.375 to 0.375
- lookup_mapping: bfloat16 [256, 256], replicated, may hold values from -0.375 to 0.375
- content_mapping: bfloat16 [256, 256], replicated, may hold values from -0.375 to 0.375
- mixing_return_matrix: bfloat16 [256, 256], replicated, may hold values from -0.375 to 0.375
- alignment_widen_map: bfloat16 [256, 1024], replicated, may hold values from -0.375 to 0.375
- alignment_shrink_map: bfloat16 [1024, 256], replicated, may hold values from -0.1875 to 0.1875
- former_embedding_map: bfloat16 [256, 32], replicated, may hold values from -0.375 to 0.375
- latter_embedding_map: bfloat16 [256, 32], replicated, may hold values from -0.375 to 0.375
- product_return_map: float32 [1024, 128], replicated, may hold values from -1 to 1
- grid_widen_map: bfloat16 [128, 512], replicated, may hold values from -0.5 to 0.5
- grid_shrink_map: bfloat16 [512, 128], replicated, may hold values from -0.25 to 0.25
Outputs:
- alignment_revised: float32 [4, 64, 256, 256], P(('groups', 'branch'), 'tile', 'col'), parts along dimension 0
- grid_revised: float32 [4, 256, 256, 128], P(('groups', 'branch'), 'tile', 'col'), parts along dimension 0
There are 2 independent parts, one for each index of `groups`. A program takes and returns all parts, laid end to end along the dimension named above; an argument that names none is the same for every part. Nothing has to cross between parts.
All inputs are finite; a program needn't handle non-finite values.
Results may differ from a plain program's by a relative error of at most 0.0075.
Values may be sent and summed in bfloat16 or wider, within the bound.
No kernel may reach another device: no remote copies, remote signals or barrier semaphores. Data moves between devices by JAX's collectives and lax.ppermute only.
A program may use at most 128 MiB of HBM per device.

v0:
```python
import jax
import jax.numpy as jnp
from jax import lax
from jax.sharding import PartitionSpec as P

SEQUENCE_DEPTH = 64


def standardize_features(x, gain):
    mean = jnp.mean(x, axis=-1, keepdims=True)
    var = jnp.mean((x - mean) ** 2, axis=-1, keepdims=True)
    return (x - mean) * lax.rsqrt(var + 1e-05) * gain


def on_device(
    alignment_tensor,
    residue_grid,
    mixing_scale_vector,
    logit_offset_scale,
    feedforward_scale,
    product_scale_vector,
    grid_scale_vector,
    logit_offset_map,
    asking_mapping,
    lookup_mapping,
    content_mapping,
    mixing_return_matrix,
    alignment_widen_map,
    alignment_shrink_map,
    former_embedding_map,
    latter_embedding_map,
    product_return_map,
    grid_widen_map,
    grid_shrink_map,
):
    sample_alignment = alignment_tensor[0]
    local_pair = residue_grid[0]
    subspace_total = logit_offset_map.shape[1]
    feature_extent = sample_alignment.shape[-1]
    subspace_number = feature_extent // subspace_total
    sequences_available = sample_alignment.shape[0]
    chain_available = sample_alignment.shape[1]
    tile_rows = local_pair.shape[0]
    tile_cols = local_pair.shape[1]
    product_extent = former_embedding_map.shape[1]
    product_operands = standardize_features(sample_alignment, product_scale_vector).astype(
        jnp.bfloat16
    )
    former_tensor = jnp.dot(
        product_operands, former_embedding_map, preferred_element_type=jnp.float32
    ).astype(jnp.bfloat16)
    latter_tensor = jnp.dot(
        product_operands, latter_embedding_map, preferred_element_type=jnp.float32
    ).astype(jnp.bfloat16)
    left_rows, right_rows = (
        lax.all_gather(former_tensor, "tile", axis=0, tiled=True),
        lax.all_gather(latter_tensor, "tile", axis=0, tiled=True),
    )
    left_all = lax.all_gather(left_rows, "col", axis=1, tiled=True)
    left_mine = lax.dynamic_slice_in_dim(left_all, lax.axis_index("tile") * tile_rows, tile_rows, 1)
    tensor_product = (
        jnp.einsum("era,eyq->ryaq", left_mine, right_rows, preferred_element_type=jnp.float32)
        / SEQUENCE_DEPTH
    )
    update = jnp.dot(
        tensor_product.reshape(tile_rows, tile_cols, product_extent * product_extent),
        product_return_map,
        precision=lax.Precision.HIGHEST,
    )
    bias_tile = jnp.einsum(
        "ijc,ch->hij",
        standardize_features(local_pair, logit_offset_scale),
        logit_offset_map,
        precision=lax.Precision.HIGHEST,
    )
    wide = lax.all_gather(bias_tile, "col", axis=2, tiled=True)
    whole = lax.all_gather(wide.astype(jnp.bfloat16), "tile", axis=1, tiled=True).astype(wide.dtype)
    bias = lax.dynamic_slice_in_dim(
        whole, lax.axis_index("col") * chain_available, chain_available, 1
    )
    standardized_source = standardize_features(sample_alignment, mixing_scale_vector).astype(
        jnp.bfloat16
    )
    asking_vectors = jnp.dot(
        standardized_source, asking_mapping, preferred_element_type=jnp.float32
    ).astype(jnp.bfloat16)
    lookup_vectors = jnp.dot(
        standardized_source, lookup_mapping, preferred_element_type=jnp.float32
    ).astype(jnp.bfloat16)
    content_vectors = jnp.dot(
        standardized_source, content_mapping, preferred_element_type=jnp.float32
    ).astype(jnp.bfloat16)
    all_keys, all_values = (
        lax.all_gather(lookup_vectors, "col", axis=1, tiled=True),
        lax.all_gather(content_vectors, "col", axis=1, tiled=True),
    )
    total_res = all_keys.shape[1]
    asking_vectors = asking_vectors.reshape(
        sequences_available, chain_available, subspace_total, subspace_number
    )
    all_keys = all_keys.reshape(sequences_available, total_res, subspace_total, subspace_number)
    all_values = all_values.reshape(sequences_available, total_res, subspace_total, subspace_number)
    scores = (
        jnp.einsum("sqhd,skhd->shqk", asking_vectors, all_keys, preferred_element_type=jnp.float32)
        / jnp.sqrt(jnp.float32(subspace_number))
        + bias[None]
    )
    weights = jax.nn.softmax(scores, axis=-1).astype(jnp.bfloat16)
    mixing_outcome = jnp.einsum(
        "shqk,skhd->sqhd", weights, all_values, preferred_element_type=jnp.float32
    )
    mixing_outcome = mixing_outcome.astype(jnp.bfloat16).reshape(
        sequences_available, chain_available, feature_extent
    )
    alignment_activations = sample_alignment + jnp.dot(
        mixing_outcome, mixing_return_matrix, preferred_element_type=jnp.float32
    )
    expanded_features = jax.nn.relu(
        jnp.dot(
            standardize_features(alignment_activations, feedforward_scale).astype(jnp.bfloat16),
            alignment_widen_map,
            preferred_element_type=jnp.float32,
        )
    ).astype(jnp.bfloat16)
    alignment_revised = alignment_activations + jnp.dot(
        expanded_features, alignment_shrink_map, preferred_element_type=jnp.float32
    )
    pair_mid = local_pair + update
    spread = jax.nn.relu(
        jnp.dot(
            standardize_features(pair_mid, grid_scale_vector).astype(jnp.bfloat16),
            grid_widen_map,
            preferred_element_type=jnp.float32,
        )
    ).astype(jnp.bfloat16)
    grid_revised = pair_mid + jnp.dot(spread, grid_shrink_map, preferred_element_type=jnp.float32)
    return (alignment_revised[None], grid_revised[None])


def solution(mesh):
    placed = (
        P(("groups", "branch"), "tile", "col", None),
        P(("groups", "branch"), "tile", "col", None),
        P(),
        P(),
        P(),
        P(),
        P(),
        P(),
        P(),
        P(),
        P(),
        P(),
        P(),
        P(),
        P(),
        P(),
        P(),
        P(),
        P(),
    )
    return jax.shard_map(
        on_device,
        mesh=mesh,
        in_specs=placed,
        out_specs=(
            P(("groups", "branch"), "tile", "col", None),
            P(("groups", "branch"), "tile", "col", None),
        ),
        check_vma=False,
    )
```

profile of v0, /device:TPU:0, one launch (start us, length us, event | category | flops | bytes accessed | tf_op | source)
XLA Modules:
  0.0 222.1 jit_solution(14404370128680419553)
XLA Ops:
  7.2 0.0 copy-start
  7.2 0.0 copy-start.2
  7.2 0.0 all-gather.11.cloned.1.call-start
  7.3 2.1 reduce_sum.89
  9.4 2.2 %multiply_reduce_fusion.3 = f32[16,128]{1,0:T(8,128)S(1)} fusion(f32[1,16,128,256]{3,2,1,0:T(8,128)} %param.19, f32[16,128]{1,0:T(8,128)S(1)} %broadcast_multiply_fusion.3), kind=kLoop, calls=%fused_computation.38 | loop fusion | flops 1570816 | bytes 2113536 | tf_op jit(solution)/shard_map/reduce_sum | solution.py:11
  11.6 0.9 convolution_convert_fusion.3
  12.6 17.4 %all_gather.26 = bf16[64,128,32]{1,2,0:T(8,128)(2,1)S(1)} all-gather(bf16[16,128,32]{1,2,0:T(8,128)(2,1)S(1)} %convolution_convert_fusion.3), channel_id=1, replica_groups=mesh['groups'=2,'tile'=4,'col'=2,'branch'=2] {'tile'}, dimensions={0}, use_global_device_ids=true | all-gather | bytes 655360 | tf_op jit(solution)/shard_map/all_gather | solution.py:56
  30.0 1.6 copy.65
  31.6 0.0 all-gather.11.cloned.1.call-update
  31.6 0.0 all-gather.9.cloned.1.call-start
  31.7 5.6 %copy.61 = f32[1,64,128,128]{2,3,1,0:T(8,128)} copy(f32[1,64,128,128]{3,2,1,0:T(8,128)} %param.20) | data formatting | bytes 8388608 | tf_op args[1]
  37.3 3.4 %reduce_sum.91 = f32[64,128]{1,0:T(8,128)S(1)} reduce(f32[1,64,128,128]{3,2,1,0:T(8,128)} %param.20, f32[]{:T(128)} %constant.17.clone.1), dimensions={0,3}, to_apply=%region_2.0 | reduce | flops 1040384 | bytes 4227076 | tf_op jit(solution)/shard_map/reduce_sum | solution.py:10
  40.7 0.0 copy-start.16
  40.7 3.5 %multiply_reduce_fusion.1 = f32[64,128]{1,0:T(8,128)S(1)} fusion(f32[1,64,128,128]{2,3,1,0:T(8,128)} %copy.61, f32[64,128]{1,0:T(8,128)S(1)} %broadcast_multiply_fusion.1), kind=kLoop, calls=%fused_computation.21 | loop fusion | flops 3137536 | bytes 4259840 | tf_op jit(solution)/shard_map/reduce_sum | solution.py:11
  44.3 0.4 copy-done.3
  44.6 2.7 %fusion.26 = bf16[8,64,128]{2,0,1:T(8,128)(2,1)S(1)} fusion(f32[1,64,128,128]{2,3,1,0:T(8,128)S(1)} %copy-done.3, f32[128]{0:T(128)S(1)} %copy-done.18, f32[64,128]{1,0:T(8,128)S(1)} %add_rsqrt_fusion.1, f32[64,128]{1,0:T(8,128)S(1)} %broadcast_multiply_fusion.1, f32[128,8]{0,1:T(8,128)S(1)} %copy-done.15), kind=kOutput, calls=%fused_computation.44 | convolution fusion | flops 103809024 | bytes 4395520 | tf_op jit(solution)/shard_map/ijc,ch->hij/dot_general | solution.py:70
  47.3 9.4 %all_gather.23 = bf16[8,64,256]{2,0,1:T(8,128)(2,1)} all-gather(bf16[8,64,128]{2,0,1:T(8,128)(2,1)S(1)} %fusion.26), channel_id=1, replica_groups=mesh['groups'=2,'tile'=4,'col'=2,'branch'=2] {'col'}, dimensions={2}, use_global_device_ids=true | all-gather | bytes 393216 | tf_op jit(solution)/shard_map/all_gather | solution.py:76
  56.7 0.0 all-gather.9.cloned.1.call-update
  56.8 0.0 all-gather.7.cloned.1.call-start
  56.8 0.7 multiply_convert_fusion.5
  57.5 0.0 copy-start.4
  57.6 1.0 copy-done.4
  58.5 1.5 convolution_convert_fusion
  60.0 0.0 all-gather.7.cloned.1.call-update
  60.0 0.0 all-gather.5.cloned.1.call-start
  60.1 2.6 %convolution_convert_fusion.2 = bf16[16,128,256]{2,1,0:T(8,128)(2,1)} fusion(bf16[16,128,256]{2,1,0:T(8,128)(2,1)} %copy-done.4, bf16[256,256]{1,0:T(8,128)(2,1)S(1)} %copy-done.9), kind=kOutput, calls=%fused_computation.43 | convolution fusion | flops 268959744 | bytes 2228224 | tf_op jit(solution)/shard_map/dot_general | solution.py:90
  62.7 0.0 all-gather.5.cloned.1.call-update
  62.8 0.9 convolution_convert_fusion.4
  63.7 16.1 %all_gather.25 = bf16[64,128,32]{1,2,0:T(8,128)(2,1)S(1)} all-gather(bf16[16,128,32]{1,2,0:T(8,128)(2,1)S(1)} %convolution_convert_fusion.4), channel_id=1, replica_groups=mesh['groups'=2,'tile'=4,'col'=2,'branch'=2] {'tile'}, dimensions={0}, use_global_device_ids=true | all-gather | bytes 655360 | tf_op jit(solution)/shard_map/all_gather | solution.py:57
  79.8 2.7 %convolution_convert_fusion.1 = bf16[16,128,256]{2,1,0:T(8,128)(2,1)} fusion(bf16[16,128,256]{2,1,0:T(8,128)(2,1)} %copy-done.4, bf16[256,256]{1,0:T(8,128)(2,1)S(1)} %copy-done.10), kind=kOutput, calls=%fused_computation.42 | convolution fusion | flops 268959744 | bytes 2228224 | tf_op jit(solution)/shard_map/dot_general | solution.py:84
  82.5 2.3 %copy.59 = bf16[16,128,256]{1,2,0:T(8,128)(2,1)} copy(bf16[16,128,256]{2,1,0:T(8,128)(2,1)} %convolution_convert_fusion.1) | data formatting | bytes 2097152 | tf_op jit(solution)/shard_map/convert_element_type | solution.py:86
  84.8 14.2 %multiply_bitcast_fusion = f32[64,128,32,32]{1,0,2,3:T(8,128)} fusion(bf16[64,128,32,1]{1,2,0,3:T(8,128)(2,1)S(1)} %bitcast.95, bf16[64,256,32]{0,1,2:T(8,128)(2,1)} %all-gather.11.cloned.1.call-done, s32[]{:T(128)S(6)} %select_n.7), kind=kOutput, calls=%fused_computation.1 | convolution fusion | flops 1082130432 | bytes 34603012 | tf_op jit(solution)/shard_map/era,eyq->ryaq/dot_general | solution.py:62
  99.1 32.0 %copy.67 = f32[64,128,32,32]{1,3,2,0:T(8,128)} copy(f32[64,128,32,32]{1,0,2,3:T(8,128)} %multiply_bitcast_fusion) | data formatting | bytes 67108864 | tf_op jit(solution)/shard_map/div | solution.py:62
  131.0 25.6 %fusion.58 = (f32[64,128]{1,0:T(8,128)S(1)}, f32[64,128,128]{1,2,0:T(8,128)}) fusion(f32[64,128,1024]{1,2,0:T(8,128)} %bitcast.94, f32[1024,128]{1,0:T(8,128)S(1)} %copy-done, f32[1,64,128,128]{2,3,1,0:T(8,128)} %copy.61), kind=kOutput, calls=%fused_computation.80 | convolution fusion | flops 12886990848 | bytes 42500096 | tf_op jit(solution)/shard_map/dot_general | solution.py:65
  156.7 3.0 %multiply_reduce_fusion = f32[64,128]{1,0:T(8,128)S(1)} fusion(f32[64,128,128]{1,2,0:T(8,128)} %get-tuple-element.15, f32[64,128]{1,0:T(8,128)S(1)} %broadcast_multiply_fusion), kind=kLoop, calls=%fused_computation.16 | loop fusion | flops 3137536 | bytes 4259840 | tf_op jit(solution)/shard_map/reduce_sum | solution.py:11
  159.8 10.1 %add_bitcast_fusion = f32[1,64,128,128]{2,3,1,0:T(8,128)} fusion(f32[64,128,128]{1,2,0:T(8,128)} %get-tuple-element.15, f32[128]{0:T(128)S(1)} %copy-done.17, f32[64,128]{1,0:T(8,128)S(1)} %add_rsqrt_fusion, f32[64,128]{1,0:T(8,128)S(1)} %broadcast_multiply_fusion, bf16[512,128]{1,0:T(8,128)(2,1)S(1)} %copy-done.6, bf16[128,512]{1,0:T(8,128)(2,1)S(1)} %copy-done.7), kind=kOutput, calls=%fused_computation.14 | convolution fusion | flops 2161115136 | bytes 8716800 | tf_op jit(solution)/shard_map/dot_general | solution.py:136
  169.9 5.6 %copy.72 = f32[1,64,128,128]{3,2,1,0:T(8,128)} copy(f32[1,64,128,128]{2,3,1,0:T(8,128)} %add_bitcast_fusion) | data formatting | bytes 8388608
  175.5 1.1 dynamic-slice_convert_fusion
  176.6 1.3 copy.63
  177.9 3.9 %copy.60 = bf16[16,256,256]{1,2,0:T(8,128)(2,1)} copy(bf16[16,256,256]{2,1,0:T(8,128)(2,1)} %all-gather.7.cloned.1.call-done) | data formatting | bytes 4194304 | tf_op jit(solution)/shard_map/all_gather | solution.py:94
  181.8 12.4 %fusion.56 = (f32[16,8,128]{2,1,0:T(8,128)S(1)}, f32[16,8,128,256]{3,2,1,0:T(8,128)}) fusion(f32[8,128,256]{2,1,0:T(8,128)} %copy.63, bf16[16,128,8,32]{1,3,2,0:T(8,128)(2,1)} %bitcast.98, bf16[16,256,8,32]{1,3,2,0:T(8,128)(2,1)} %bitcast.96), kind=kOutput, calls=%fused_computation.78 | convolution fusion | flops 285212928 | bytes 21037056 | tf_op jit(solution)/shard_map/sub | solution.py:108
  194.2 3.9 %copy.58 = bf16[16,256,256]{1,2,0:T(8,128)(2,1)} copy(bf16[16,256,256]{2,1,0:T(8,128)(2,1)} %all-gather.5.cloned.1.call-done) | data formatting | bytes 4194304 | tf_op jit(solution)/shard_map/all_gather | solution.py:95
  198.1 8.3 %fusion.25 = bf16[16,8,32,128]{3,2,1,0:T(8,128)(2,1)S(1)} fusion(bf16[16,256,8,32]{1,3,2,0:T(8,128)(2,1)} %bitcast.97, f32[16,8,128,256]{3,2,1,0:T(8,128)} %get-tuple-element.11, f32[16,8,128]{2,1,0:T(8,128)S(1)} %get-tuple-element.10), kind=kOutput, calls=%fused_computation.40 | convolution fusion | flops 277348352 | bytes 19988480 | tf_op jit(solution)/shard_map/shqk,skhd->sqhd/dot_general | solution.py:109
  206.5 0.8 fusion.57
  207.3 1.3 copy-done.5
  208.6 0.6 multiply_reduce_fusion.2
  209.3 0.0 copy-start.1
  209.3 6.3 %add_bitcast_fusion.1 = f32[1,16,128,256]{3,2,1,0:T(8,128)} fusion(f32[16,128,256]{2,1,0:T(8,128)} %copy-done.5, f32[256]{0:T(256)S(1)} %copy-done.20, f32[16,128]{1,0:T(8,128)S(1)} %add_rsqrt_fusion.2, f32[16,128]{1,0:T(8,128)S(1)} %broadcast_multiply_fusion.2, bf16[1024,256]{1,0:T(8,128)(2,1)S(1)} %copy-done.19, bf16[256,1024]{1,0:T(8,128)(2,1)} %param.31), kind=kOutput, calls=%fused_computation.31 | convolution fusion | flops 2154299392 | bytes 5260288 | tf_op jit(solution)/shard_map/dot_general | solution.py:125
  (46 shorter events, 0.1 us)
Async XLA Ops:
  7.2 123.9 %copy-start = (f32[1024,128]{1,0:T(8,128)S(1)}, f32[1024,128]{1,0:T(8,128)}, u32[]{:S(2)}) copy-start(f32[1024,128]{1,0:T(8,128)} %param.35) | copy-start | bytes 1572868
  7.2 4.4 %copy-start.2 = (f32[1,16,128,256]{3,2,1,0:T(8,128)S(1)}, f32[1,16,128,256]{3,2,1,0:T(8,128)}, u32[]{:S(2)}) copy-start(f32[1,16,128,256]{3,2,1,0:T(8,128)} %param.19) | copy-start | bytes 6291460
  7.2 4.4 %copy-start.14 = (f32[256]{0:T(256)S(1)}, f32[256]{0:T(256)}, u32[]{:S(2)}) copy-start(f32[256]{0:T(256)} %param.24) | copy-start | bytes 3076
  7.2 4.4 %copy-start.12 = (bf16[256,32]{0,1:T(8,128)(2,1)S(1)}, bf16[256,32]{0,1:T(8,128)(2,1)}, u32[]{:S(2)}) copy-start(bf16[256,32]{0,1:T(8,128)(2,1)} %param.33) | copy-start | bytes 49156
  7.2 77.6 %all-gather.11.cloned.1.call-start = ((), (), s32[]{:S(2)}) async-start(), calls=%async_computation.3 | async-start | bytes 3145728 | tf_op jit(solution)/shard_map/all_gather | solution.py:59
  31.6 143.9 %all-gather.9.cloned.1.call-start = ((), (), s32[]{:S(2)}) async-start(), calls=%async_computation.2 | async-start | bytes 1310720 | tf_op jit(solution)/shard_map/all_gather | solution.py:77
  37.3 7.0 %copy-start.15 = (f32[128,8]{0,1:T(8,128)S(1)}, f32[128,8]{0,1:T(8,128)}, u32[]{:S(2)}) copy-start(f32[128,8]{0,1:T(8,128)} %param.26) | copy-start | bytes 12292
  37.3 7.0 %copy-start.18 = (f32[128]{0:T(128)S(1)}, f32[128]{0:T(128)}, u32[]{:S(2)}) copy-start(f32[128]{0:T(128)} %param.22) | copy-start | bytes 1540
  40.7 3.9 %copy-start.3 = (f32[1,64,128,128]{2,3,1,0:T(8,128)S(1)}, f32[1,64,128,128]{2,3,1,0:T(8,128)}, u32[]{:S(2)}) copy-start(f32[1,64,128,128]{2,3,1,0:T(8,128)} %copy.61) | copy-start | bytes 12582916
  40.7 16.1 %copy-start.16 = (f32[256]{0:T(256)S(1)}, f32[256]{0:T(256)}, u32[]{:S(2)}) copy-start(f32[256]{0:T(256)} %param.21) | copy-start | bytes 3076
  44.2 14.3 %copy-start.8 = (bf16[256,256]{1,0:T(8,128)(2,1)S(1)}, bf16[256,256]{1,0:T(8,128)(2,1)}, u32[]{:S(2)}) copy-start(bf16[256,256]{1,0:T(8,128)(2,1)} %param.28) | copy-start | bytes 393220
  47.3 12.7 %copy-start.9 = (bf16[256,256]{1,0:T(8,128)(2,1)S(1)}, bf16[256,256]{1,0:T(8,128)(2,1)}, u32[]{:S(2)}) copy-start(bf16[256,256]{1,0:T(8,128)(2,1)} %param.29) | copy-start | bytes 393220
  56.7 6.0 %copy-start.13 = (bf16[256,32]{0,1:T(8,128)(2,1)S(1)}, bf16[256,32]{0,1:T(8,128)(2,1)}, u32[]{:S(2)}) copy-start(bf16[256,32]{0,1:T(8,128)(2,1)} %param.34) | copy-start | bytes 49156
  56.8 121.2 %all-gather.7.cloned.1.call-start = ((), (), s32[]{:S(2)}) async-start(), calls=%async_computation.1 | async-start | bytes 3145728 | tf_op jit(solution)/shard_map/all_gather | solution.py:94
  57.5 1.0 copy-start.4
  60.0 19.8 %copy-start.10 = (bf16[256,256]{1,0:T(8,128)(2,1)S(1)}, bf16[256,256]{1,0:T(8,128)(2,1)}, u32[]{:S(2)}) copy-start(bf16[256,256]{1,0:T(8,128)(2,1)} %param.27) | copy-start | bytes 393220
  60.0 134.2 %all-gather.5.cloned.1.call-start = ((), (), s32[]{:S(2)}) async-start(), calls=%async_computation | async-start | bytes 3145728 | tf_op jit(solution)/shard_map/all_gather | solution.py:95
  156.7 3.1 %copy-start.6 = (bf16[512,128]{1,0:T(8,128)(2,1)S(1)}, bf16[512,128]{1,0:T(8,128)(2,1)}, u32[]{:S(2)}) copy-start(bf16[512,128]{1,0:T(8,128)(2,1)} %param.37) | copy-start | bytes 393220
  156.7 3.1 %copy-start.7 = (bf16[128,512]{1,0:T(8,128)(2,1)S(1)}, bf16[128,512]{1,0:T(8,128)(2,1)}, u32[]{:S(2)}) copy-start(bf16[128,512]{1,0:T(8,128)(2,1)} %param.36) | copy-start | bytes 393220
  156.7 3.1 %copy-start.17 = (f32[128]{0:T(128)S(1)}, f32[128]{0:T(128)}, u32[]{:S(2)}) copy-start(f32[128]{0:T(128)} %param.25) | copy-start | bytes 1540
  198.1 8.4 %copy-start.11 = (bf16[256,256]{1,0:T(8,128)(2,1)S(1)}, bf16[256,256]{1,0:T(8,128)(2,1)}, u32[]{:S(2)}) copy-start(bf16[256,256]{1,0:T(8,128)(2,1)} %param.30) | copy-start | bytes 393220
  206.4 2.8 %copy-start.19 = (bf16[1024,256]{1,0:T(8,128)(2,1)S(1)}, bf16[1024,256]{1,0:T(8,128)(2,1)}, u32[]{:S(2)}) copy-start(bf16[1024,256]{1,0:T(8,128)(2,1)} %param.32) | copy-start | bytes 1572868
  206.5 2.8 %copy-start.20 = (f32[256]{0:T(256)S(1)}, f32[256]{0:T(256)}, u32[]{:S(2)}) copy-start(f32[256]{0:T(256)} %param.23) | copy-start | bytes 3076
  207.3 1.4 copy-start.5
  209.3 6.3 %copy-start.1 = (f32[1024,128]{1,0:T(8,128)S(1)}, f32[1024,128]{1,0:T(8,128)}, u32[]{:S(2)}) copy-start(f32[1024,128]{1,0:T(8,128)} %param.35) | copy-start | bytes 1572868
Sparse Core Ops, SparseCore 0:
  31.7 37.6 all-gather.10
  71.0 27.9 all-gather.8
  100.6 32.5 all-gather.6
  134.6 33.0 all-gather.4
where the time goes:
time: 223 us; the launch traced here: 222 us
  matrix products  89.1 us (40%)
  local copies, waits for them, and re-layouts  59 us (26%)
  blocking collectives  42.9 us (19%)
  other arithmetic  16.8 us (8%)
  between operations  14.1 us (6%)
    div x1, local copies, waits for them, and re-layouts, on_device(): jnp.einsum('era,eyq->ryaq', left_mine, right_rows, preferred_element_type...  32 us
    dot_general x1, matrix products, on_device(): jnp.dot(tensor_product.reshape(tile_rows, tile_cols, product_extent * pro...  25.6 us
    all_gather x1, blocking collectives, on_device(): lax.all_gather(former_tensor, 'tile', axis=0, tiled=True)  17.4 us
    all_gather x1, blocking collectives, on_device(): lax.all_gather(latter_tensor, 'tile', axis=0, tiled=True)  16.1 us
    dot_general x1, matrix products, on_device(): jnp.einsum('era,eyq->ryaq', left_mine, right_rows, preferred_element_type...  14.2 us
    unnamed x44, local copies, waits for them, and re-layouts  14 us
    sub x1, matrix products, on_device(): weights = jax.nn.softmax(scores, axis=-1).astype(jnp.bfloat16)  12.4 us
    dot_general x1, matrix products, on_device(): jnp.dot(spread, grid_shrink_map, preferred_element_type=jnp.float32)  10.1 us
  transfers between devices with their start and end apart: 4, of which 0 were waited for; matrix products, arithmetic and copies ran while one was open for 61% of the time, Pallas kernels for 0%

commit v1 on v0

--- a/solution.py
+++ b/solution.py
@@ -53,7 +53,15 @@
         product_operands, latter_embedding_map, preferred_element_type=jnp.float32
     ).astype(jnp.bfloat16)
     left_rows, right_rows = (
-        lax.all_gather(former_tensor, "tile", axis=0, tiled=True),
+        jnp.concatenate(
+            lax.all_to_all(
+                jnp.stack([former_tensor] * lax.axis_size("tile")),
+                axis_name="tile",
+                split_axis=0,
+                concat_axis=0,
+            ),
+            axis=0,
+        ),
         lax.all_gather(latter_tensor, "tile", axis=0, tiled=True),
     )
     left_all = lax.all_gather(left_rows, "col", axis=1, tiled=True)

time: 223 us -> 237 us (1.063)
  blocking collectives: 42.9 us -> 53.5 us
  waiting for transfers between devices: 0.07 us -> 7.37 us
  other arithmetic: 16.8 us -> 13.1 us
    all_to_all x0 -> x1, blocking collectives: none -> 30.5 us  [on_device(): lax.all_to_all(jnp.stack([former_tensor] * lax.axis_size('tile')), axis_n...]
    all_gather x1 -> x0, blocking collectives: 17.4 us -> none  [on_device(): lax.all_gather(former_tensor, 'tile', axis=0, tiled=True)]
    all_gather x1, waiting for transfers between devices: 0.01 us -> 7.3 us  [on_device(): left_all = lax.all_gather(left_rows, 'col', axis=1, tiled=True)]
  transfers between devices with their start and end apart: 4 -> 4, of which waited for: 0 -> 1; matrix products, arithmetic and copies ran while one was open for 61% -> 53% of each run, Pallas kernels for 0% -> 0%
where the time goes in v1:
time: 237 us
  matrix products  89.6 us (38%)
  local copies, waits for them, and re-layouts  58.7 us (25%)
  blocking collectives  53.5 us (23%)
  between operations  14.1 us (6%)
  other arithmetic  13.1 us (6%)
  waiting for transfers between devices  7.37 us (3%)
    div x1, local copies, waits for them, and re-layouts, on_device(): jnp.einsum('era,eyq->ryaq', left_mine, right_rows, preferred_element_type...  31.7 us
    all_to_all x1, blocking collectives, on_device(): lax.all_to_all(jnp.stack([former_tensor] * lax.axis_size('tile')), axis_n...  30.5 us
    dot_general x1, matrix products, on_device(): jnp.dot(tensor_product.reshape(tile_rows, tile_cols, product_extent * pro...  25.6 us
    all_gather x1, blocking collectives, on_device(): lax.all_gather(latter_tensor, 'tile', axis=0, tiled=True)  15.7 us
    dot_general x1, matrix products, on_device(): jnp.einsum('era,eyq->ryaq', left_mine, right_rows, preferred_element_type...  15.1 us
    unnamed x44, local copies, waits for them, and re-layouts  13.8 us
    sub x1, matrix products, on_device(): weights = jax.nn.softmax(scores, axis=-1).astype(jnp.bfloat16)  12.4 us
    dot_general x1, matrix products, on_device(): jnp.dot(spread, grid_shrink_map, preferred_element_type=jnp.float32)  10.1 us
  transfers between devices with their start and end apart: 4, of which 1 were waited for; matrix products, arithmetic and copies ran while one was open for 53% of the time, Pallas kernels for 0%

profile of v1, /device:TPU:0, one launch (start us, length us, event | category | flops | bytes accessed | tf_op | source)
XLA Modules:
  0.0 236.6 jit_solution(18209784090632360822)
XLA Ops:
  7.2 0.0 copy-start
  7.2 0.0 all-gather.9.cloned.1.call-start
  7.2 5.6 %copy.63 = f32[1,64,128,128]{2,3,1,0:T(8,128)} copy(f32[1,64,128,128]{3,2,1,0:T(8,128)} %param.20) | data formatting | bytes 8388608 | tf_op args[1]
  12.9 3.4 %reduce_sum.91 = f32[64,128]{1,0:T(8,128)S(1)} reduce(f32[1,64,128,128]{3,2,1,0:T(8,128)} %param.20, f32[]{:T(128)} %constant.17.clone.1), dimensions={0,3}, to_apply=%region_2.0 | reduce | flops 1040384 | bytes 4227076 | tf_op jit(solution)/shard_map/reduce_sum | solution.py:10
  16.2 0.0 copy-start.3
  16.3 3.2 %multiply_reduce_fusion.1 = f32[64,128]{1,0:T(8,128)S(1)} fusion(f32[1,64,128,128]{2,3,1,0:T(8,128)} %copy.63, f32[64,128]{1,0:T(8,128)S(1)} %broadcast_multiply_fusion.1), kind=kLoop, calls=%fused_computation.21 | loop fusion | flops 3137536 | bytes 4259840 | tf_op jit(solution)/shard_map/reduce_sum | solution.py:11
  19.5 0.2 copy-done.3
  19.7 2.7 %fusion.26 = bf16[8,64,128]{2,0,1:T(8,128)(2,1)S(1)} fusion(f32[1,64,128,128]{2,3,1,0:T(8,128)S(1)} %copy-done.3, f32[128]{0:T(128)S(1)} %copy-done.18, f32[64,128]{1,0:T(8,128)S(1)} %add_rsqrt_fusion.1, f32[64,128]{1,0:T(8,128)S(1)} %broadcast_multiply_fusion.1, f32[128,8]{0,1:T(8,128)S(1)} %copy-done.15), kind=kOutput, calls=%fused_computation.44 | convolution fusion | flops 103809024 | bytes 4395520 | tf_op jit(solution)/shard_map/ijc,ch->hij/dot_general | solution.py:78
  22.4 7.2 %all_gather.20 = bf16[8,64,256]{2,0,1:T(8,128)(2,1)} all-gather(bf16[8,64,128]{2,0,1:T(8,128)(2,1)S(1)} %fusion.26), channel_id=1, replica_groups=mesh['groups'=2,'tile'=4,'col'=2,'branch'=2] {'col'}, dimensions={2}, use_global_device_ids=true | all-gather | bytes 393216 | tf_op jit(solution)/shard_map/all_gather | solution.py:84
  29.7 0.0 all-gather.9.cloned.1.call-update
  29.7 0.0 all-gather.11.cloned.1.call-start
  29.7 0.3 reduce_sum.89
  30.1 0.6 multiply_reduce_fusion.3
  30.8 0.9 convolution_convert_fusion.3
  31.8 0.1 stack.2
  31.8 30.5 %all_to_all.5 = bf16[4,16,128,32]{2,3,1,0:T(8,128)(2,1)S(1)} all-to-all(bf16[4,16,128,32]{2,3,1,0:T(8,128)(2,1)S(1)} %stack.2), channel_id=1, replica_groups=mesh['groups'=2,'tile'=4,'col'=2,'branch'=2] {'tile'}, dimensions={0} | all-to-all | bytes 1048576 | tf_op jit(solution)/shard_map/all_to_all | solution.py:57
  62.4 1.6 copy.67
  64.0 0.0 all-gather.11.cloned.1.call-update
  64.0 0.0 all-gather.7.cloned.1.call-start
  64.1 0.7 multiply_convert_fusion.5
  64.8 1.0 copy-done.4
  65.8 1.5 convolution_convert_fusion
  67.3 0.0 all-gather.7.cloned.1.call-update
  67.3 0.0 all-gather.5.cloned.1.call-start
  67.3 2.6 %convolution_convert_fusion.2 = bf16[16,128,256]{2,1,0:T(8,128)(2,1)} fusion(bf16[16,128,256]{2,1,0:T(8,128)(2,1)} %copy-done.4, bf16[256,256]{1,0:T(8,128)(2,1)S(1)} %copy-done.9), kind=kOutput, calls=%fused_computation.43 | convolution fusion | flops 268959744 | bytes 2228224 | tf_op jit(solution)/shard_map/dot_general | solution.py:98
  70.0 0.0 all-gather.5.cloned.1.call-update
  70.0 0.9 convolution_convert_fusion.4
  71.0 15.7 %all_gather.22 = bf16[64,128,32]{1,2,0:T(8,128)(2,1)S(1)} all-gather(bf16[16,128,32]{1,2,0:T(8,128)(2,1)S(1)} %convolution_convert_fusion.4), channel_id=1, replica_groups=mesh['groups'=2,'tile'=4,'col'=2,'branch'=2] {'tile'}, dimensions={0}, use_global_device_ids=true | all-gather | bytes 655360 | tf_op jit(solution)/shard_map/all_gather | solution.py:65
  86.7 2.6 %convolution_convert_fusion.1 = bf16[16,128,256]{2,1,0:T(8,128)(2,1)} fusion(bf16[16,128,256]{2,1,0:T(8,128)(2,1)} %copy-done.4, bf16[256,256]{1,0:T(8,128)(2,1)S(1)} %copy-done.10), kind=kOutput, calls=%fused_computation.42 | convolution fusion | flops 268959744 | bytes 2228224 | tf_op jit(solution)/shard_map/dot_general | solution.py:92
  89.3 2.3 copy.61
  91.6 1.1 dynamic-slice_convert_fusion
  92.7 1.3 copy.65
  94.1 7.3 %all-gather.11.cloned.1.call-done = bf16[64,256,32]{0,1,2:T(8,128)(2,1)} async-done(((bf16[64,128,32]{0,1,2:T(8,128)(2,1)}), bf16[64,256,32]{0,1,2:T(8,128)(2,1)}) %all-gather.11.cloned.1.call-update) | async-done | bytes 1048592 | tf_op jit(solution)/shard_map/all_gather | solution.py:67
  101.4 15.1 %multiply_bitcast_fusion = f32[64,128,32,32]{1,0,2,3:T(8,128)} fusion(bf16[64,128,32,1]{1,2,0,3:T(8,128)(2,1)S(1)} %bitcast.96, bf16[64,256,32]{0,1,2:T(8,128)(2,1)} %all-gather.11.cloned.1.call-done, s32[]{:T(128)S(6)} %select_n.7), kind=kOutput, calls=%fused_computation.1 | convolution fusion | flops 1082130432 | bytes 34603012 | tf_op jit(solution)/shard_map/era,eyq->ryaq/dot_general | solution.py:70
  116.5 31.7 %copy.69 = f32[64,128,32,32]{1,3,2,0:T(8,128)} copy(f32[64,128,32,32]{1,0,2,3:T(8,128)} %multiply_bitcast_fusion) | data formatting | bytes 67108864 | tf_op jit(solution)/shard_map/div | solution.py:70
  148.2 25.6 %fusion.58 = (f32[64,128]{1,0:T(8,128)S(1)}, f32[64,128,128]{1,2,0:T(8,128)}) fusion(f32[64,128,1024]{1,2,0:T(8,128)} %bitcast.95, f32[1024,128]{1,0:T(8,128)S(1)} %copy-done, f32[1,64,128,128]{2,3,1,0:T(8,128)} %copy.63), kind=kOutput, calls=%fused_computation.80 | convolution fusion | flops 12886990848 | bytes 42500096 | tf_op jit(solution)/shard_map/dot_general | solution.py:73
  173.8 3.0 %multiply_reduce_fusion = f32[64,128]{1,0:T(8,128)S(1)} fusion(f32[64,128,128]{1,2,0:T(8,128)} %get-tuple-element.15, f32[64,128]{1,0:T(8,128)S(1)} %broadcast_multiply_fusion), kind=kLoop, calls=%fused_computation.16 | loop fusion | flops 3137536 | bytes 4259840 | tf_op jit(solution)/shard_map/reduce_sum | solution.py:11
  176.9 10.1 %add_bitcast_fusion = f32[1,64,128,128]{2,3,1,0:T(8,128)} fusion(f32[64,128,128]{1,2,0:T(8,128)} %get-tuple-element.15, f32[128]{0:T(128)S(1)} %copy-done.17, f32[64,128]{1,0:T(8,128)S(1)} %add_rsqrt_fusion, f32[64,128]{1,0:T(8,128)S(1)} %broadcast_multiply_fusion, bf16[512,128]{1,0:T(8,128)(2,1)S(1)} %copy-done.6, bf16[128,512]{1,0:T(8,128)(2,1)S(1)} %copy-done.7), kind=kOutput, calls=%fused_computation.14 | convolution fusion | flops 2161115136 | bytes 8716800 | tf_op jit(solution)/shard_map/dot_general | solution.py:144
  187.0 5.6 %copy.74 = f32[1,64,128,128]{3,2,1,0:T(8,128)} copy(f32[1,64,128,128]{2,3,1,0:T(8,128)} %add_bitcast_fusion) | data formatting | bytes 8388608
  192.6 3.9 %copy.62 = bf16[16,256,256]{1,2,0:T(8,128)(2,1)} copy(bf16[16,256,256]{2,1,0:T(8,128)(2,1)} %all-gather.7.cloned.1.call-done) | data formatting | bytes 4194304 | tf_op jit(solution)/shard_map/all_gather | solution.py:102
  196.5 12.4 %fusion.56 = (f32[16,8,128]{2,1,0:T(8,128)S(1)}, f32[16,8,128,256]{3,2,1,0:T(8,128)}) fusion(f32[8,128,256]{2,1,0:T(8,128)} %copy.65, bf16[16,128,8,32]{1,3,2,0:T(8,128)(2,1)} %bitcast.100, bf16[16,256,8,32]{1,3,2,0:T(8,128)(2,1)} %bitcast.98), kind=kOutput, calls=%fused_computation.78 | convolution fusion | flops 285212928 | bytes 21037056 | tf_op jit(solution)/shard_map/sub | solution.py:116
  208.9 3.9 %copy.60 = bf16[16,256,256]{1,2,0:T(8,128)(2,1)} copy(bf16[16,256,256]{2,1,0:T(8,128)(2,1)} %all-gather.5.cloned.1.call-done) | data formatting | bytes 4194304 | tf_op jit(solution)/shard_map/all_gather | solution.py:103
  212.8 8.1 %fusion.25 = bf16[16,8,32,128]{3,2,1,0:T(8,128)(2,1)S(1)} fusion(bf16[16,256,8,32]{1,3,2,0:T(8,128)(2,1)} %bitcast.99, f32[16,8,128,256]{3,2,1,0:T(8,128)} %get-tuple-element.11, f32[16,8,128]{2,1,0:T(8,128)S(1)} %get-tuple-element.10), kind=kOutput, calls=%fused_computation.40 | convolution fusion | flops 277348352 | bytes 19988480 | tf_op jit(solution)/shard_map/shqk,skhd->sqhd/dot_general | solution.py:117
  220.9 0.0 copy-start.19
  220.9 0.8 fusion.57
  221.7 1.3 copy-done.5
  223.1 0.6 multiply_reduce_fusion.2
  223.8 6.3 %add_bitcast_fusion.1 = f32[1,16,128,256]{3,2,1,0:T(8,128)} fusion(f32[16,128,256]{2,1,0:T(8,128)} %copy-done.5, f32[256]{0:T(256)S(1)} %copy-done.20, f32[16,128]{1,0:T(8,128)S(1)} %add_rsqrt_fusion.2, f32[16,128]{1,0:T(8,128)S(1)} %broadcast_multiply_fusion.2, bf16[1024,256]{1,0:T(8,128)(2,1)S(1)} %copy-done.19, bf16[256,1024]{1,0:T(8,128)(2,1)} %param.31), kind=kOutput, calls=%fused_computation.31 | convolution fusion | flops 2154299392 | bytes 5260288 | tf_op jit(solution)/shard_map/dot_general | solution.py:133
  (47 shorter events, 0.1 us)
Async XLA Ops:
  7.2 141.1 %copy-start = (f32[1024,128]{1,0:T(8,128)S(1)}, f32[1024,128]{1,0:T(8,128)}, u32[]{:S(2)}) copy-start(f32[1024,128]{1,0:T(8,128)} %param.35) | copy-start | bytes 1572868
  7.2 84.4 %all-gather.9.cloned.1.call-start = ((), (), s32[]{:S(2)}) async-start(), calls=%async_computation.3 | async-start | bytes 1310720 | tf_op jit(solution)/shard_map/all_gather | solution.py:85
  12.9 6.6 %copy-start.15 = (f32[128,8]{0,1:T(8,128)S(1)}, f32[128,8]{0,1:T(8,128)}, u32[]{:S(2)}) copy-start(f32[128,8]{0,1:T(8,128)} %param.26) | copy-start | bytes 12292
  12.9 6.6 %copy-start.18 = (f32[128]{0:T(128)S(1)}, f32[128]{0:T(128)}, u32[]{:S(2)}) copy-start(f32[128]{0:T(128)} %param.22) | copy-start | bytes 1540
  16.2 3.5 %copy-start.3 = (f32[1,64,128,128]{2,3,1,0:T(8,128)S(1)}, f32[1,64,128,128]{2,3,1,0:T(8,128)}, u32[]{:S(2)}) copy-start(f32[1,64,128,128]{2,3,1,0:T(8,128)} %copy.63) | copy-start | bytes 12582916
  16.3 13.5 %copy-start.2 = (f32[1,16,128,256]{3,2,1,0:T(8,128)S(1)}, f32[1,16,128,256]{3,2,1,0:T(8,128)}, u32[]{:S(2)}) copy-start(f32[1,16,128,256]{3,2,1,0:T(8,128)} %param.19) | copy-start | bytes 6291460
  19.7 11.1 %copy-start.12 = (bf16[256,32]{0,1:T(8,128)(2,1)S(1)}, bf16[256,32]{0,1:T(8,128)(2,1)}, u32[]{:S(2)}) copy-start(bf16[256,32]{0,1:T(8,128)(2,1)} %param.33) | copy-start | bytes 49156
  19.7 11.1 %copy-start.14 = (f32[256]{0:T(256)S(1)}, f32[256]{0:T(256)}, u32[]{:S(2)}) copy-start(f32[256]{0:T(256)} %param.24) | copy-start | bytes 3076
  29.7 71.7 %all-gather.11.cloned.1.call-start = ((), (), s32[]{:S(2)}) async-start(), calls=%async_computation.4 | async-start | bytes 3145728 | tf_op jit(solution)/shard_map/all_gather | solution.py:67
  30.1 34.0 %copy-start.16 = (f32[256]{0:T(256)S(1)}, f32[256]{0:T(256)}, u32[]{:S(2)}) copy-start(f32[256]{0:T(256)} %param.21) | copy-start | bytes 3076
  31.8 34.0 %copy-start.8 = (bf16[256,256]{1,0:T(8,128)(2,1)S(1)}, bf16[256,256]{1,0:T(8,128)(2,1)}, u32[]{:S(2)}) copy-start(bf16[256,256]{1,0:T(8,128)(2,1)} %param.28) | copy-start | bytes 393220
  62.4 5.0 %copy-start.9 = (bf16[256,256]{1,0:T(8,128)(2,1)S(1)}, bf16[256,256]{1,0:T(8,128)(2,1)}, u32[]{:S(2)}) copy-start(bf16[256,256]{1,0:T(8,128)(2,1)} %param.29) | copy-start | bytes 393220
  64.0 6.0 %copy-start.13 = (bf16[256,32]{0,1:T(8,128)(2,1)S(1)}, bf16[256,32]{0,1:T(8,128)(2,1)}, u32[]{:S(2)}) copy-start(bf16[256,32]{0,1:T(8,128)(2,1)} %param.34) | copy-start | bytes 49156
  64.0 128.6 %all-gather.7.cloned.1.call-start = ((), (), s32[]{:S(2)}) async-start(), calls=%async_computation.2 | async-start | bytes 3145728 | tf_op jit(solution)/shard_map/all_gather | solution.py:102
  64.8 1.0 copy-start.4
  67.3 19.4 %copy-start.10 = (bf16[256,256]{1,0:T(8,128)(2,1)S(1)}, bf16[256,256]{1,0:T(8,128)(2,1)}, u32[]{:S(2)}) copy-start(bf16[256,256]{1,0:T(8,128)(2,1)} %param.27) | copy-start | bytes 393220
  67.3 141.6 %all-gather.5.cloned.1.call-start = ((), (), s32[]{:S(2)}) async-start(), calls=%async_computation.1 | async-start | bytes 3145728 | tf_op jit(solution)/shard_map/all_gather | solution.py:103
  173.8 3.1 %copy-start.6 = (bf16[512,128]{1,0:T(8,128)(2,1)S(1)}, bf16[512,128]{1,0:T(8,128)(2,1)}, u32[]{:S(2)}) copy-start(bf16[512,128]{1,0:T(8,128)(2,1)} %param.37) | copy-start | bytes 393220
  173.8 3.1 %copy-start.7 = (bf16[128,512]{1,0:T(8,128)(2,1)S(1)}, bf16[128,512]{1,0:T(8,128)(2,1)}, u32[]{:S(2)}) copy-start(bf16[128,512]{1,0:T(8,128)(2,1)} %param.36) | copy-start | bytes 393220
  173.8 3.1 %copy-start.17 = (f32[128]{0:T(128)S(1)}, f32[128]{0:T(128)}, u32[]{:S(2)}) copy-start(f32[128]{0:T(128)} %param.25) | copy-start | bytes 1540
  212.8 8.1 %copy-start.11 = (bf16[256,256]{1,0:T(8,128)(2,1)S(1)}, bf16[256,256]{1,0:T(8,128)(2,1)}, u32[]{:S(2)}) copy-start(bf16[256,256]{1,0:T(8,128)(2,1)} %param.30) | copy-start | bytes 393220
  220.9 2.8 %copy-start.19 = (bf16[1024,256]{1,0:T(8,128)(2,1)S(1)}, bf16[1024,256]{1,0:T(8,128)(2,1)}, u32[]{:S(2)}) copy-start(bf16[1024,256]{1,0:T(8,128)(2,1)} %param.32) | copy-start | bytes 1572868
  220.9 2.8 %copy-start.20 = (f32[256]{0:T(256)S(1)}, f32[256]{0:T(256)}, u32[]{:S(2)}) copy-start(f32[256]{0:T(256)} %param.23) | copy-start | bytes 3076
  221.7 1.4 copy-start.5
  223.7 6.3 %copy-start.1 = (f32[1024,128]{1,0:T(8,128)S(1)}, f32[1024,128]{1,0:T(8,128)}, u32[]{:S(2)}) copy-start(f32[1024,128]{1,0:T(8,128)} %param.35) | copy-start | bytes 1572868
Sparse Core Ops, SparseCore 0:
  29.8 37.7 all-gather.8
  69.2 32.1 all-gather.10
  102.9 33.0 all-gather.6
  137.5 33.0 all-gather.4
